TPU v7x, 256 devices: a whole 4x4x8 slice. The times are simulated.
256 devices in a mesh: row: 16 (over z, core), col: 4 (over x), inner: 4 (over y).
Axes of the slice: x: 4, y: 4, z: 8, core: 2. Of those that a mesh axis runs over, the one named last changes fastest.
Arguments:
- density: bfloat16 [64, 16, 256, 256], P('row', ('col', 'inner')), may hold values from -1.5 to 1.5, as said below
- block_cols: int32 [64, 16], replicated, may hold values from 0 to 63, as said below
- mixing: float32 [3], replicated, may hold values from 0.02 to 1.5, as said below
Outputs:
- purified: bfloat16 [64, 16, 256, 256], P('row', ('col', 'inner'))
Inputs may be any that keep to these rules, and one draw needn't show every extreme that they name: Slot g of block row i names a block row of group g (rows g * 4 to g * 4 + 3); within one group of block rows, slot g names each row of group g once. Slot i // 4 of row i names i itself. The pattern is symmetric: row block_cols[i, g] names i in slot i // 4. It is consistent: block_cols[block_cols[i, t], g] == block_cols[i, g] for all i, t, g. `density`: block (i, g) is the transpose of block (block_cols[i, g], i // 4). `mixing`: element 0 lies in 0.5 to 1.5, elements 1 and 2 in 0.02 to 0.05.
All inputs are finite; a program needn't handle non-finite values.
Results may differ from a plain program's by a relative error of at most 0.007.
Values may be sent and summed in bfloat16 or wider, within the bound.
No kernel may reach another device: no remote copies, remote signals or barrier semaphores. Data moves between devices by JAX's collectives and lax.ppermute only.
A program may use at most 128 MiB of HBM per device.

v0:
```python
import jax
import jax.numpy as jnp
from jax import lax
from jax.sharding import PartitionSpec as P

GS = 4


def laid_out(tiles, dim):
    tiles = jnp.moveaxis(tiles, 0, dim)
    shape = tiles.shape
    return tiles.reshape(*shape[:dim], shape[dim] * shape[dim + 1], *shape[dim + 2 :])


def from_everyone(shard, axis):
    size = lax.axis_size(axis)
    return lax.all_to_all(
        jnp.broadcast_to(shard[None], (size, *shard.shape)), axis, 0, 0, tiled=True
    )


def gathered_copies(shard, axis, dim):
    return laid_out(from_everyone(shard, axis), dim)


def fold_with(panel, piece):
    return jnp.einsum("htab,tgbc->hgac", panel, piece, preferred_element_type=jnp.float32)


def clique_filter(density, block_cols, mixing, row_start):
    row_count = density.shape[0]
    width = density.shape[2]
    groups_here = row_count // GS
    first_group = row_start // GS
    leaders = lax.dynamic_slice_in_dim(block_cols[:GS], first_group, groups_here, 1)
    ordered = density[:, 0][(leaders - row_start).reshape(-1)]
    ordered = ordered.reshape(GS, groups_here, 1, width, width)
    arrived = lax.all_to_all(ordered, "inner", split_axis=0, concat_axis=2, tiled=True)
    blocks = arrived[0]
    slot_count = blocks.shape[1]
    slot_start = lax.axis_index("col") * slot_count
    density_panel = gathered_copies(blocks, "col", 1)
    square = fold_with(density_panel, lax.all_gather(blocks, "row", axis=0, tiled=True)).astype(
        jnp.bfloat16
    )
    group_ids = first_group + jnp.arange(groups_here, dtype=jnp.int32)
    slot_ids = slot_start + jnp.arange(slot_count, dtype=jnp.int32)
    on_diagonal = (group_ids[:, None] == slot_ids[None, :]).astype(jnp.float32)
    identity = jnp.eye(width, dtype=jnp.float32)
    mixer_blocks = (
        mixing[0] * on_diagonal[:, :, None, None] * identity
        + mixing[1] * blocks.astype(jnp.float32)
        + mixing[2] * square.astype(jnp.float32)
    ).astype(jnp.bfloat16)
    square_panel = gathered_copies(square, "col", 1)
    filtered = fold_with(
        square_panel, lax.all_gather(mixer_blocks, "row", axis=0, tiled=True)
    ).astype(jnp.bfloat16)
    returned = lax.all_to_all(filtered[None], "inner", split_axis=2, concat_axis=0, tiled=True)
    regrouped = returned.reshape(GS * groups_here, 1, width, width)
    local_rows = row_start + jnp.arange(row_count, dtype=jnp.int32)
    clique_ids = lax.dynamic_slice_in_dim(block_cols[:, 0], row_start, row_count, 0)
    positions = clique_ids * groups_here + (local_rows // GS - first_group)
    return regrouped[positions]


def body(density, block_cols, mixing):
    row_count = density.shape[0]
    row_start = lax.axis_index("row") * row_count
    return clique_filter(density, block_cols, mixing, row_start)


def solution(mesh):
    in_specs = (P("row", ("col", "inner"), None, None), P(), P())
    out_specs = P("row", ("col", "inner"), None, None)
    return jax.shard_map(body, mesh=mesh, in_specs=in_specs, out_specs=out_specs, check_vma=False)
```

profile of v0, /device:TPU:1, one launch (start us, length us, event | category | flops | bytes accessed | tf_op | source)
XLA Modules:
  0.0 174.0 jit_solution(14277715915551514343)
XLA Ops:
  6.5 0.8 fusion.6
  7.3 0.3 copy-done
  7.6 0.6 gather_fusion
  8.2 0.2 copy.15
  8.4 13.4 %all_to_all.28 = bf16[4,1,1,256,256]{3,4,2,1,0:T(8,128)(2,1)S(1)} all-to-all(bf16[4,1,1,256,256]{3,4,2,1,0:T(8,128)(2,1)S(1)} %copy.15), channel_id=1, replica_groups=mesh['row'=16,'col'=4,'inner'=4] {'inner'}, dimensions={0} | all-to-all | bytes 1048576 | tf_op jit(solution)/shard_map/all_to_all | solution.py:38
  21.8 1.0 copy.17
  22.8 0.2 copy.18
  23.0 1.6 broadcast_in_dim.11
  24.6 4.1 %all-to-all-start.1 = ((bf16[4,1,4,256,256]{4,3,2,1,0:T(8,128)(2,1)}), bf16[4,1,4,256,256]{4,3,2,1,0:T(8,128)(2,1)S(1)}, u32[]{:S(2)}, u32[]{:S(2)}) async-start(bf16[4,1,4,256,256]{4,3,2,1,0:T(8,128)(2,1)} %broadcast_in_dim.11), calls=%async_computation.1 | async-start | bytes 4194304 | tf_op jit(solution)/shard_map/all_to_all | solution.py:17
  28.8 0.6 fusion.8
  29.4 0.6 compare_select_fusion.2
  30.0 23.1 %all-to-all-done.1 = bf16[4,1,4,256,256]{4,3,2,1,0:T(8,128)(2,1)S(1)} async-done(((bf16[4,1,4,256,256]{4,3,2,1,0:T(8,128)(2,1)}), bf16[4,1,4,256,256]{4,3,2,1,0:T(8,128)(2,1)S(1)}, u32[]{:S(2)}, u32[]{:S(2)}) %all-to-all-start.1) | async-done | bytes 2097184 | tf_op jit(solution)/shard_map/all_to_all | solution.py:17
  53.1 28.2 %all-gather.6.cloned.1.call-done = bf16[64,1,1,256,256]{4,3,2,1,0:T(8,128)(2,1)} async-done(((bf16[4,1,1,256,256]{4,3,2,1,0:T(8,128)(2,1)}), bf16[64,1,1,256,256]{4,3,2,1,0:T(8,128)(2,1)}) %all-gather.6.cloned.1.call-update) | async-done | bytes 8388624 | tf_op jit(solution)/shard_map/all_gather | solution.py:43
  81.3 8.0 %fusion.4 = (bf16[1,4,256,256]{2,3,1,0:T(8,128)(2,1)}, bf16[4,256,256]{2,1,0:T(8,128)(2,1)}) fusion(bf16[4,1,1,256,256]{3,4,2,1,0:T(8,128)(2,1)S(1)} %all_to_all.28, f32[]{:T(128)} %bitcast.1, f32[]{:T(128)} %bitcast.7, f32[256,256]{0,1:T(8,128)S(1)} %fusion.5, f32[4]{0:T(128)S(1)} %compare_select_fusion.2, bf16[16,4,256,256]{3,2,1,0:T(8,128)(2,1)} %bitcast.69, ...), kind=kOutput, calls=%fused_computation.9 | convolution fusion | flops 2149842944 | bytes 12320792 | tf_op jit(solution)/shard_map/htab,tgbc->hgac/dot_general | solution.py:27
  89.3 2.1 %copy.20 = bf16[1,4,256,256]{3,2,1,0:T(8,128)(2,1)} copy(bf16[1,4,256,256]{2,3,1,0:T(8,128)(2,1)} %get-tuple-element.8) | data formatting | bytes 1048576 | tf_op jit(solution)/shard_map/convert_element_type | solution.py:54
  91.4 1.2 copy.21
  92.9 29.6 %all_to_all.29 = bf16[4,1,4,256,256]{4,3,2,1,0:T(8,128)(2,1)S(1)} all-to-all(bf16[4,1,4,256,256]{4,3,2,1,0:T(8,128)(2,1)S(1)} %broadcast_in_dim.26), channel_id=1, replica_groups=mesh['row'=16,'col'=4,'inner'=4] {'col'}, dimensions={0} | all-to-all | bytes 4194304 | tf_op jit(solution)/shard_map/all_to_all | solution.py:17
  122.5 23.5 %all-gather.4.cloned.1.call-done = bf16[16,4,256,256]{3,2,1,0:T(8,128)(2,1)} async-done(((bf16[1,4,256,256]{3,2,1,0:T(8,128)(2,1)}), bf16[16,4,256,256]{3,2,1,0:T(8,128)(2,1)}) %all-gather.4.cloned.1.call-update) | async-done | bytes 8388624 | tf_op jit(solution)/shard_map/all_gather | solution.py:57
  146.0 6.5 %fusion.2 = bf16[1,1,4,256,256]{3,4,1,0,2:T(8,128)(2,1)} fusion(bf16[16,4,256,256]{3,2,1,0:T(8,128)(2,1)} %all-gather.4.cloned.1.call-done, bf16[16,256,256,1]{2,1,3,0:T(8,128)(2,1)S(1)} %bitcast.63), kind=kOutput, calls=%fused_computation.6 | convolution fusion | flops 2147745792 | bytes 11010048 | tf_op jit(solution)/shard_map/htab,tgbc->hgac/dot_general | solution.py:27
  152.5 4.0 %all-to-all-start.3 = ((bf16[1,1,4,256,256]{3,4,1,0,2:T(8,128)(2,1)}), bf16[1,1,4,256,256]{3,4,1,0,2:T(8,128)(2,1)S(1)}, u32[]{:S(2)}, u32[]{:S(2)}) async-start(bf16[1,1,4,256,256]{3,4,1,0,2:T(8,128)(2,1)} %fusion.2), calls=%async_computation.3 | async-start | bytes 1048576 | tf_op jit(solution)/shard_map/all_to_all | solution.py:59
  156.5 0.7 slice.19
  157.3 8.2 %all-to-all-done.3 = bf16[1,1,4,256,256]{3,4,1,0,2:T(8,128)(2,1)S(1)} async-done(((bf16[1,1,4,256,256]{3,4,1,0,2:T(8,128)(2,1)}), bf16[1,1,4,256,256]{3,4,1,0,2:T(8,128)(2,1)S(1)}, u32[]{:S(2)}, u32[]{:S(2)}) %all-to-all-start.3) | async-done | bytes 524320 | tf_op jit(solution)/shard_map/all_to_all | solution.py:59
  165.6 0.6 gather_fusion.1
  166.1 1.0 copy.24
  (12 shorter events, 0.4 us)
Async XLA Ops:
  6.5 1.1 copy-start
  6.5 74.8 %all-gather.6.cloned.1.call-start = ((), (), s32[]{:S(2)}) async-start(), calls=%async_computation.5 | async-start | bytes 8912896 | tf_op jit(solution)/shard_map/all_gather | solution.py:43
  24.6 4.2 %copy-start.1 = (f32[3]{0:T(128)S(1)}, f32[3]{0:T(128)}, u32[]{:S(2)}) copy-start(f32[3]{0:T(128)} %param.5) | copy-start | bytes 40
  24.6 28.5 %all-to-all-start.1 = ((bf16[4,1,4,256,256]{4,3,2,1,0:T(8,128)(2,1)}), bf16[4,1,4,256,256]{4,3,2,1,0:T(8,128)(2,1)S(1)}, u32[]{:S(2)}, u32[]{:S(2)}) async-start(bf16[4,1,4,256,256]{4,3,2,1,0:T(8,128)(2,1)} %broadcast_in_dim.11), calls=%async_computation.1 | async-start | bytes 4194304 | tf_op jit(solution)/shard_map/all_to_all | solution.py:17
  28.8 117.2 %all-gather.4.cloned.1.call-start = ((), (), s32[]{:S(2)}) async-start(), calls=%async_computation.4 | async-start | bytes 8912896 | tf_op jit(solution)/shard_map/all_gather | solution.py:57
  152.5 13.0 %all-to-all-start.3 = ((bf16[1,1,4,256,256]{3,4,1,0,2:T(8,128)(2,1)}), bf16[1,1,4,256,256]{3,4,1,0,2:T(8,128)(2,1)S(1)}, u32[]{:S(2)}, u32[]{:S(2)}) async-start(bf16[1,1,4,256,256]{3,4,1,0,2:T(8,128)(2,1)} %fusion.2), calls=%async_computation.3 | async-start | bytes 1048576 | tf_op jit(solution)/shard_map/all_to_all | solution.py:59
Sparse Core Ops, SparseCore 0:
  23.0 58.3 all-gather.5
  91.5 54.3 all-gather.3
where the time goes:
time: 175 us; the launch traced here: 174 us
  waiting for transfers between devices  83 us (47%)
  blocking collectives  43.1 us (25%)
  matrix products  14.6 us (8%)
  between operations  13.5 us (8%)
  local copies, waits for them, and re-layouts  10.2 us (6%)
  starting transfers between devices  8.15 us (5%)
    all_to_all x1, blocking collectives, from_everyone(): lax.all_to_all(jnp.broadcast_to(shard[None], (size, *shard.shape)), axis,...  29.6 us
    all_gather x1, waiting for transfers between devices, clique_filter(): lax.all_gather(blocks, 'row', axis=0, tiled=True)  28.2 us
    all_gather x1, waiting for transfers between devices, clique_filter(): lax.all_gather(mixer_blocks, 'row', axis=0, tiled=True)  23.5 us
    all_to_all x1, waiting for transfers between devices, from_everyone(): lax.all_to_all(jnp.broadcast_to(shard[None], (size, *shard.shape)), axis,...  23.1 us
    dot_general x2, matrix products, fold_with(): jnp.einsum('htab,tgbc->hgac', panel, piece, preferred_element_type=jnp.fl...  14.6 us
    all_to_all x1, blocking collectives, clique_filter(): lax.all_to_all(ordered, 'inner', split_axis=0, concat_axis=2, tiled=True)  13.4 us
    all_to_all x1, waiting for transfers between devices, clique_filter(): lax.all_to_all(filtered[None], 'inner', split_axis=2, concat_axis=0, tile...  8.25 us
    all_to_all x1, starting transfers between devices, from_everyone(): lax.all_to_all(jnp.broadcast_to(shard[None], (size, *shard.shape)), axis,...  4.14 us
  transfers between devices with their start and end apart: 4, of which 4 were waited for; matrix products, arithmetic and copies ran while one was open for 3% of the time, Pallas kernels for 0%

commit v1 on v0

--- a/solution.py
+++ b/solution.py
@@ -1,9 +1,23 @@
+import functools
 import jax
 import jax.numpy as jnp
 from jax import lax
 from jax.sharding import PartitionSpec as P
+from jax.lax import all_to_all, psum
 
 GS = 4
+
+
+def _rest_sheet(x_in, in_dim):
+    return jnp.concatenate(
+        all_to_all(
+            jnp.stack([x_in] * psum(1, axis_name="row"), axis=0), "row", split_axis=0, concat_axis=0
+        ),
+        axis=in_dim,
+    )
+
+
+define_points = functools.partial(_rest_sheet, in_dim=0)
 
 
 def laid_out(tiles, dim):
@@ -40,9 +54,7 @@
     slot_count = blocks.shape[1]
     slot_start = lax.axis_index("col") * slot_count
     density_panel = gathered_copies(blocks, "col", 1)
-    square = fold_with(density_panel, lax.all_gather(blocks, "row", axis=0, tiled=True)).astype(
-        jnp.bfloat16
-    )
+    square = fold_with(density_panel, define_points(blocks)).astype(jnp.bfloat16)
     group_ids = first_group + jnp.arange(groups_here, dtype=jnp.int32)
     slot_ids = slot_start + jnp.arange(slot_count, dtype=jnp.int32)
     on_diagonal = (group_ids[:, None] == slot_ids[None, :]).astype(jnp.float32)

time: 175 us -> 340 us (1.94)
  waiting for transfers between devices: 83 us -> 213 us
  blocking collectives: 43.1 us -> 69.2 us
  starting transfers between devices: 8.15 us -> 15.9 us
    all_to_all x1, waiting for transfers between devices: 23.1 us -> 182 us  [_rest_sheet(): all_to_all(jnp.stack([x_in] * psum(1, axis_name='row'), axis=0), 'row', s...]
    all_gather x1 -> x0, waiting for transfers between devices: 28.2 us -> none  [clique_filter(): lax.all_gather(blocks, 'row', axis=0, tiled=True)]
    all_to_all x1 -> x2, blocking collectives: 29.6 us -> 55.8 us  [from_everyone(): lax.all_to_all(jnp.broadcast_to(shard[None], (size, *shard.shape)), axis,...]
    all_to_all x1, starting transfers between devices: 4.14 us -> 11.8 us  [_rest_sheet(): all_to_all(jnp.stack([x_in] * psum(1, axis_name='row'), axis=0), 'row', s...]
    another operation x0 -> x1, local copies, waits for them, and re-layouts: none -> 4.26 us  [_rest_sheet(): jnp.stack([x_in] * psum(1, axis_name='row'), axis=0)]
  transfers between devices with their start and end apart: 4 -> 3, of which waited for: 4 -> 3; matrix products, arithmetic and copies ran while one was open for 3% -> 1% of each run, Pallas kernels for 0% -> 0%
where the time goes in v1:
time: 340 us
  waiting for transfers between devices  213 us (63%)
  blocking collectives  69.2 us (20%)
  starting transfers between devices  15.9 us (5%)
  matrix products  14.5 us (4%)
  between operations  13.5 us (4%)
  local copies, waits for them, and re-layouts  12.2 us (4%)
    all_to_all x1, waiting for transfers between devices, _rest_sheet(): all_to_all(jnp.stack([x_in] * psum(1, axis_name='row'), axis=0), 'row', s...  182 us
    all_to_all x2, blocking collectives, from_everyone(): lax.all_to_all(jnp.broadcast_to(shard[None], (size, *shard.shape)), axis,...  55.8 us
    all_gather x1, waiting for transfers between devices, clique_filter(): lax.all_gather(mixer_blocks, 'row', axis=0, tiled=True)  22.6 us
    dot_general x2, matrix products, fold_with(): jnp.einsum('htab,tgbc->hgac', panel, piece, preferred_element_type=jnp.fl...  14.5 us
    all_to_all x1, blocking collectives, clique_filter(): lax.all_to_all(ordered, 'inner', split_axis=0, concat_axis=2, tiled=True)  13.4 us
    all_to_all x1, starting transfers between devices, _rest_sheet(): all_to_all(jnp.stack([x_in] * psum(1, axis_name='row'), axis=0), 'row', s...  11.8 us
    all_to_all x1, waiting for transfers between devices, clique_filter(): lax.all_to_all(filtered[None], 'inner', split_axis=2, concat_axis=0, tile...  8.25 us
  transfers between devices with their start and end apart: 3, of which 3 were waited for; matrix products, arithmetic and copies ran while one was open for 1% of the time, Pallas kernels for 0%

profile of v1, /device:TPU:1, one launch (start us, length us, event | category | flops | bytes accessed | tf_op | source)
XLA Modules:
  0.0 339.6 jit_solution(7860372055999071410)
XLA Ops:
  6.5 0.8 fusion.14
  7.3 0.3 copy-done
  7.6 0.6 gather_fusion
  8.2 0.2 copy.13
  8.4 13.4 %all_to_all.36 = bf16[4,1,1,256,256]{3,4,2,1,0:T(8,128)(2,1)S(1)} all-to-all(bf16[4,1,1,256,256]{3,4,2,1,0:T(8,128)(2,1)S(1)} %copy.13), channel_id=1, replica_groups=mesh['row'=16,'col'=4,'inner'=4] {'inner'}, dimensions={0} | all-to-all | bytes 1048576 | tf_op jit(solution)/shard_map/all_to_all | solution.py:52
  21.8 0.2 copy.16
  22.0 0.2 broadcast_in_dim.8
  22.2 27.9 %all_to_all.37 = bf16[4,1,4,256,256]{4,3,2,1,0:T(8,128)(2,1)S(1)} all-to-all(bf16[4,1,4,256,256]{4,3,2,1,0:T(8,128)(2,1)S(1)} %broadcast_in_dim.8), channel_id=1, replica_groups=mesh['row'=16,'col'=4,'inner'=4] {'col'}, dimensions={0} | all-to-all | bytes 4194304 | tf_op jit(solution)/shard_map/all_to_all | solution.py:31
  50.1 4.3 %stack.3 = bf16[16,1,4,256,256]{3,4,2,1,0:T(8,128)(2,1)} broadcast(bf16[4,256,256]{1,2,0:T(8,128)(2,1)S(1)} %bitcast.68), dimensions={2,3,4} | broadcast | bytes 8912896 | tf_op jit(solution)/shard_map/stack | solution.py:14
  54.3 11.8 %all-to-all-start.1 = ((bf16[16,1,4,256,256]{3,4,2,1,0:T(8,128)(2,1)}), bf16[16,1,4,256,256]{3,4,2,1,0:T(8,128)(2,1)}, u32[]{:S(2)}, u32[]{:S(2)}) async-start(bf16[16,1,4,256,256]{3,4,2,1,0:T(8,128)(2,1)} %stack.3), calls=%async_computation.1 | async-start | bytes 16777216 | tf_op jit(solution)/shard_map/all_to_all | solution.py:13
  66.3 0.6 fusion.16
  66.9 0.6 compare_select_fusion.2
  67.6 182.0 %all-to-all-done.1 = bf16[16,1,4,256,256]{3,4,2,1,0:T(8,128)(2,1)} async-done(((bf16[16,1,4,256,256]{3,4,2,1,0:T(8,128)(2,1)}), bf16[16,1,4,256,256]{3,4,2,1,0:T(8,128)(2,1)}, u32[]{:S(2)}, u32[]{:S(2)}) %all-to-all-start.1) | async-done | bytes 8388640 | tf_op jit(solution)/shard_map/all_to_all | solution.py:13
  249.6 8.0 %fusion.12 = (bf16[1,4,256,256]{2,3,1,0:T(8,128)(2,1)}, bf16[4,256,256]{2,1,0:T(8,128)(2,1)}) fusion(bf16[4,1,1,256,256]{3,4,2,1,0:T(8,128)(2,1)S(1)} %all_to_all.36, f32[]{:T(128)} %bitcast.7, f32[]{:T(128)} %bitcast.1, f32[256,256]{0,1:T(8,128)S(1)} %fusion.13, f32[4]{0:T(128)S(1)} %compare_select_fusion.2, bf16[16,256,256,1]{2,1,0,3:T(8,128)(2,1)S(1)} %bitcast.69, ...), kind=kOutput, calls=%fused_computation.12 | convolution fusion | flops 2149842944 | bytes 12320792 | tf_op jit(solution)/shard_map/htab,tgbc->hgac/dot_general | solution.py:41
  257.6 2.1 copy.17
  259.7 1.2 copy.18
  261.1 27.9 %all_to_all.38 = bf16[4,1,4,256,256]{4,3,2,1,0:T(8,128)(2,1)S(1)} all-to-all(bf16[4,1,4,256,256]{4,3,2,1,0:T(8,128)(2,1)S(1)} %broadcast_in_dim.10), channel_id=1, replica_groups=mesh['row'=16,'col'=4,'inner'=4] {'col'}, dimensions={0} | all-to-all | bytes 4194304 | tf_op jit(solution)/shard_map/all_to_all | solution.py:31
  289.1 22.6 %all-gather.2.cloned.1.call-done = bf16[16,4,256,256]{3,2,1,0:T(8,128)(2,1)} async-done(((bf16[1,4,256,256]{3,2,1,0:T(8,128)(2,1)}), bf16[16,4,256,256]{3,2,1,0:T(8,128)(2,1)}) %all-gather.2.cloned.1.call-update) | async-done | bytes 8388624 | tf_op jit(solution)/shard_map/all_gather | solution.py:69
  311.6 6.6 %fusion.10 = bf16[1,1,4,256,256]{3,4,1,0,2:T(8,128)(2,1)} fusion(bf16[16,4,256,256]{3,2,1,0:T(8,128)(2,1)} %all-gather.2.cloned.1.call-done, bf16[16,256,256,1]{2,1,3,0:T(8,128)(2,1)S(1)} %bitcast.70), kind=kOutput, calls=%fused_computation.9 | convolution fusion | flops 2147745792 | bytes 11010048 | tf_op jit(solution)/shard_map/htab,tgbc->hgac/dot_general | solution.py:41
  318.2 4.0 %all-to-all-start.4 = ((bf16[1,1,4,256,256]{3,4,1,0,2:T(8,128)(2,1)}), bf16[1,1,4,256,256]{3,4,1,0,2:T(8,128)(2,1)S(1)}, u32[]{:S(2)}, u32[]{:S(2)}) async-start(bf16[1,1,4,256,256]{3,4,1,0,2:T(8,128)(2,1)} %fusion.10), calls=%async_computation.4 | async-start | bytes 1048576 | tf_op jit(solution)/shard_map/all_to_all | solution.py:71
  322.2 0.7 slice.19
  322.9 8.2 %all-to-all-done.4 = bf16[1,1,4,256,256]{3,4,1,0,2:T(8,128)(2,1)S(1)} async-done(((bf16[1,1,4,256,256]{3,4,1,0,2:T(8,128)(2,1)}), bf16[1,1,4,256,256]{3,4,1,0,2:T(8,128)(2,1)S(1)}, u32[]{:S(2)}, u32[]{:S(2)}) %all-to-all-start.4) | async-done | bytes 524320 | tf_op jit(solution)/shard_map/all_to_all | solution.py:71
  331.2 0.6 gather_fusion.1
  331.8 1.0 copy.21
  (10 shorter events, 0.4 us)
Async XLA Ops:
  6.5 1.1 copy-start
  54.3 11.9 %copy-start.1 = (f32[3]{0:T(128)S(1)}, f32[3]{0:T(128)}, u32[]{:S(2)}) copy-start(f32[3]{0:T(128)} %param.5) | copy-start | bytes 40
  54.3 195.2 %all-to-all-start.1 = ((bf16[16,1,4,256,256]{3,4,2,1,0:T(8,128)(2,1)}), bf16[16,1,4,256,256]{3,4,2,1,0:T(8,128)(2,1)}, u32[]{:S(2)}, u32[]{:S(2)}) async-start(bf16[16,1,4,256,256]{3,4,2,1,0:T(8,128)(2,1)} %stack.3), calls=%async_computation.1 | async-start | bytes 16777216 | tf_op jit(solution)/shard_map/all_to_all | solution.py:13
  66.2 245.4 %all-gather.2.cloned.1.call-start = ((), (), s32[]{:S(2)}) async-start(), calls=%async_computation.5 | async-start | bytes 8912896 | tf_op jit(solution)/shard_map/all_gather | solution.py:69
  318.2 13.0 %all-to-all-start.4 = ((bf16[1,1,4,256,256]{3,4,1,0,2:T(8,128)(2,1)}), bf16[1,1,4,256,256]{3,4,1,0,2:T(8,128)(2,1)S(1)}, u32[]{:S(2)}, u32[]{:S(2)}) async-start(bf16[1,1,4,256,256]{3,4,1,0,2:T(8,128)(2,1)} %fusion.10), calls=%async_computation.4 | async-start | bytes 1048576 | tf_op jit(solution)/shard_map/all_to_all | solution.py:71
Sparse Core Ops, SparseCore 0:
  259.8 51.7 all-gather.1
